TPU v7x, 128 devices: a whole 4x4x4 slice. The times are simulated.
128 devices in a mesh: dp: 32 (over z, y_hi, x), tensor: 4 (over y_lo, core).
Axes of the slice: x: 4, y: 4 (y_hi: 2, y_lo: 2; y = y_hi * 2 + y_lo), z: 4, core: 2. Of those that a mesh axis runs over, the one named last changes fastest.
Arguments:
- tokens: bfloat16 [32, 4, 128, 2048], P('dp', 'tensor'), may hold values from -6 to 6
- doc_ids: int32 [32, 4, 128], P('dp'), may hold values from 0 to 3, never falling along the last dimension, each value on 1 to 64 neighbouring positions
- attn_gain: float32 [2048], P(('dp', 'tensor')), may hold values from 0.5 to 1.5
- forget_floor: float32 [2048], P(('dp', 'tensor')), may hold values from 0.5 to 0.98
- w_query: bfloat16 [2048, 2048], P('dp', 'tensor'), may hold values from -0.125 to 0.125
- w_forget: bfloat16 [2048, 2048], P('dp', 'tensor'), may hold values from -0.125 to 0.125
- w_value: bfloat16 [2048, 2048], P('dp', 'tensor'), may hold values from -0.125 to 0.125
- w_outgate: bfloat16 [2048, 2048], P('dp', 'tensor'), may hold values from -0.125 to 0.125
- w_output: bfloat16 [2048, 2048], P('tensor', 'dp'), may hold values from -0.125 to 0.125
- mlp_gain: float32 [2048], P(('dp', 'tensor')), may hold values from 0.5 to 1.5
- w_gate: bfloat16 [2048, 5632], P('dp', 'tensor'), may hold values from -0.125 to 0.125
- w_up: bfloat16 [2048, 5632], P('dp', 'tensor'), may hold values from -0.125 to 0.125
- w_down: bfloat16 [5632, 2048], P('tensor', 'dp'), may hold values from -0.078125 to 0.078125
- cotangent: bfloat16 [32, 4, 128, 2048], P('dp', 'tensor'), may hold values from -6 to 6
Outputs:
- layer_out: bfloat16 [32, 4, 128, 2048], P('dp', 'tensor')
- grad_tokens: float32 [32, 4, 128, 2048], P('dp', 'tensor')
- grad_attn_gain: float32 [2048], P(('dp', 'tensor'))
- grad_floor: float32 [2048], P(('dp', 'tensor'))
- grad_query: float32 [2048, 2048], P('dp', 'tensor')
- grad_forget: float32 [2048, 2048], P('dp', 'tensor')
- grad_value: float32 [2048, 2048], P('dp', 'tensor')
- grad_outgate: float32 [2048, 2048], P('dp', 'tensor')
- grad_output: float32 [2048, 2048], P('tensor', 'dp')
- grad_mlp_gain: float32 [2048], P(('dp', 'tensor'))
- grad_gate: float32 [2048, 5632], P('dp', 'tensor')
- grad_up: float32 [2048, 5632], P('dp', 'tensor')
- grad_down: float32 [5632, 2048], P('tensor', 'dp')
Inputs may be any that keep to these rules, and one draw needn't show every extreme that they name: `doc_ids`: within each row of 128 tokens the sequence numbers never fall; each sequence has 1 to 64 tokens, and the longest has exactly 64.
All inputs are finite; a program needn't handle non-finite values.
Results may differ from a plain program's by a relative error of at most 0.025.
Values may be sent and summed in bfloat16 or wider, within the bound.
No kernel may reach another device: no remote copies, remote signals or barrier semaphores. Data moves between devices by JAX's collectives and lax.ppermute only.
A program may use at most 192 MiB of HBM per device.

v0:
```python
import jax
import jax.numpy as jnp
from jax import lax
from jax.sharding import PartitionSpec as P

HK = 128
HIGHEST = lax.Precision.HIGHEST
epsilon = 1e-06


def row_scale(values):
    return lax.rsqrt(jnp.mean(values * values, axis=-1, keepdims=True) + epsilon)


def silu_slope(values):
    sigmoid_val = jax.nn.sigmoid(values)
    return sigmoid_val * (1.0 + values * (1.0 - sigmoid_val))


def matmul_plain(left, right):
    return jnp.dot(left, right, preferred_element_type=jnp.float32)


def times_trans(left, right):
    return lax.dot_general(
        left, right, (((1,), (1,)), ((), ())), preferred_element_type=jnp.float32
    )


def trans_times(left, right):
    return lax.dot_general(
        left, right, (((0,), (0,)), ((), ())), preferred_element_type=jnp.float32
    )


def recurrence(query, forget_raw, value, floor_vec, doc_rows):
    length = query.shape[1]
    forget = floor_vec + (1.0 - floor_vec) * jax.nn.sigmoid(forget_raw)
    log_forget = jnp.log(forget)
    keyed = 1.0 - forget
    position = jnp.arange(length)
    same_doc = doc_rows[:, :, None] == doc_rows[:, None, :]
    causal = same_doc & (position[:, None] >= position[None, :])
    starts = jnp.concatenate(
        [jnp.zeros_like(doc_rows[:, :1], dtype=bool), doc_rows[:, 1:] == doc_rows[:, :-1]], axis=1
    )
    summing = (causal & starts[:, None, :]).astype(jnp.float32)
    running = jnp.einsum("rij,rjhk->rihk", summing, log_forget, precision=HIGHEST)
    query_t = query * jnp.exp(running)
    key_t = keyed * jnp.exp(-running)
    scores = jnp.einsum("rihk,rjhk->rhij", query_t, key_t, precision=HIGHEST)
    scores = jnp.where(causal[:, None], scores, 0.0)
    return jnp.einsum("rhij,rjhv->rihv", scores, value, precision=HIGHEST)


ON_CHIP = [(0, 1), (1, 0), (2, 3), (3, 2)]
ACROSS = [(0, 2), (2, 0), (1, 3), (3, 1)]
SLOT_XOR = (0, 2, 1, 3)


def row_gather(values):
    across = lax.ppermute(values, "tensor", ACROSS)
    pair = jnp.stack([values, across])
    other = lax.ppermute(pair, "tensor", ON_CHIP)
    return jnp.concatenate([pair, other]).reshape((-1,) + values.shape[1:])


def row_sum(values):
    blocks = values.reshape((4, -1) + values.shape[1:])
    got = lax.ppermute(blocks[2:], "tensor", ON_CHIP)
    mine = blocks[0] + got[0]
    theirs = blocks[1] + got[1]
    return mine + lax.ppermute(theirs, "tensor", ACROSS)


def spread_sum(values, axis, count):
    blocks = values.reshape((count, -1) + values.shape[1:])
    got = lax.all_to_all(blocks, axis, 0, 0, tiled=False)
    return got.astype(jnp.float32).sum(axis=0)


def small_gather(vectors):
    count = 128
    spread = jnp.broadcast_to(vectors[None], (count,) + vectors.shape)
    got = lax.all_to_all(spread, ("dp", "tensor"), 0, 0, tiled=False)
    return jnp.swapaxes(got, 0, 1).reshape(vectors.shape[0], -1)


def small_sum(vectors):
    count = 128
    blocks = vectors.reshape(vectors.shape[0], count, -1)
    got = lax.all_to_all(jnp.swapaxes(blocks, 0, 1), ("dp", "tensor"), 0, 0, tiled=False)
    return got.sum(axis=0)


def shards(
    tokens,
    doc_ids,
    attn_gain,
    forget_floor,
    w_query,
    w_forget,
    w_value,
    w_outgate,
    w_output,
    mlp_gain,
    w_gate,
    w_up,
    w_down,
    cotangent,
):
    gains = small_gather(jnp.stack([attn_gain, forget_floor, mlp_gain]))
    attn_full, floor_full, mlp_full = (gains[0], gains[1], gains[2])
    part_index = lax.axis_index("tensor")
    local_width = w_query.shape[1]
    local_heads = local_width // HK
    hidden_width = w_gate.shape[1]
    floor_local = lax.dynamic_slice_in_dim(
        floor_full, part_index * local_width, local_width
    ).reshape(local_heads, HK)
    model_width = attn_full.shape[0]
    slot_rows = jnp.bitwise_xor(part_index, jnp.array(SLOT_XOR, jnp.int32))
    doc_all = jnp.take(doc_ids[0], slot_rows, axis=0)
    row_count = doc_all.shape[0]
    resid_in = tokens[0].reshape(-1, model_width).astype(jnp.float32)
    cot_local = cotangent[0].reshape(-1, model_width)
    attn_pack = jnp.concatenate([w_query, w_forget, w_value, w_outgate, w_output.T], axis=1)
    mlp_pack = jnp.concatenate([w_gate, w_up, w_down.T], axis=1)
    attn_all = lax.all_gather(attn_pack, "dp", axis=0, tiled=True)
    mlp_all = lax.all_gather(mlp_pack, "dp", axis=0, tiled=True)
    wq_all = attn_all[:, 0 * local_width : 1 * local_width]
    wf_all = attn_all[:, 1 * local_width : 2 * local_width]
    wv_all = attn_all[:, 2 * local_width : 3 * local_width]
    wg_all = attn_all[:, 3 * local_width : 4 * local_width]
    wo_t = attn_all[:, 4 * local_width : 5 * local_width]
    wgate_all = mlp_all[:, 0:hidden_width]
    wup_all = mlp_all[:, hidden_width : 2 * hidden_width]
    wdown_t = mlp_all[:, 2 * hidden_width : 3 * hidden_width]
    scale_one = row_scale(resid_in)
    normed = row_gather((resid_in * scale_one * attn_full).astype(jnp.bfloat16))
    query = matmul_plain(normed, wq_all)
    forget_raw = matmul_plain(normed, wf_all)
    value = matmul_plain(normed, wv_all)
    out_gate = matmul_plain(normed, wg_all)

    def mixer(query_in, forget_in, value_in, floor_in):

        def shaped(arr):
            return arr.reshape(row_count, -1, local_heads, HK)

        mixed_rows = recurrence(
            shaped(query_in), shaped(forget_in), shaped(value_in), floor_in, doc_all
        )
        return mixed_rows.reshape(query_in.shape[0], local_width)

    mixed, pullback = jax.vjp(mixer, query, forget_raw, value, floor_local)
    gate_act = jax.nn.silu(out_gate)
    gated = (mixed * gate_act).astype(jnp.bfloat16)
    branch = row_sum(times_trans(gated, wo_t))
    resid = resid_in + branch
    scale_two = row_scale(resid)
    normed2 = row_gather((resid * scale_two * mlp_full).astype(jnp.bfloat16))
    gate_proj = matmul_plain(normed2, wgate_all)
    up_proj = matmul_plain(normed2, wup_all)
    gate_silu = jax.nn.silu(gate_proj)
    hidden = (gate_silu * up_proj).astype(jnp.bfloat16)
    ffn_out = row_sum(times_trans(hidden, wdown_t))
    layer_out = (resid + ffn_out).astype(jnp.bfloat16).reshape(tokens.shape)
    cot_full = row_gather(cot_local)
    d_hidden = matmul_plain(cot_full, wdown_t)
    grad_down_t = trans_times(cot_full, hidden)
    d_gate = (d_hidden * up_proj * silu_slope(gate_proj)).astype(jnp.bfloat16)
    d_up = (d_hidden * gate_silu).astype(jnp.bfloat16)
    grad_gate = trans_times(normed2, d_gate)
    grad_up = trans_times(normed2, d_up)
    mlp_grads = jnp.concatenate(
        [
            grad_gate.astype(jnp.bfloat16),
            grad_up.astype(jnp.bfloat16),
            grad_down_t.astype(jnp.bfloat16),
        ],
        axis=1,
    )
    mlp_red = lax.psum_scatter(mlp_grads, "dp", scatter_dimension=0, tiled=True).astype(jnp.float32)
    d_normed2 = row_sum(times_trans(d_gate, wgate_all) + times_trans(d_up, wup_all))
    grad_mlp = jnp.sum(d_normed2 * resid * scale_two, axis=0)
    inner_two = jnp.mean(d_normed2 * mlp_full * resid, axis=-1, keepdims=True)
    d_resid = (
        cot_local.astype(jnp.float32)
        + d_normed2 * mlp_full * scale_two
        - resid * scale_two**3 * inner_two
    )
    d_branch = row_gather(d_resid.astype(jnp.bfloat16))
    d_gated = matmul_plain(d_branch, wo_t)
    grad_output_t = trans_times(d_branch, gated)
    d_mixed = d_gated * gate_act
    d_outgate = (d_gated * mixed * silu_slope(out_gate)).astype(jnp.bfloat16)
    d_query, d_forget, d_value, d_floor = pullback(d_mixed)
    d_query = d_query.astype(jnp.bfloat16)
    d_forget = d_forget.astype(jnp.bfloat16)
    d_value = d_value.astype(jnp.bfloat16)
    grad_query = trans_times(normed, d_query)
    grad_forget = trans_times(normed, d_forget)
    grad_value = trans_times(normed, d_value)
    grad_outgate = trans_times(normed, d_outgate)
    attn_grads = jnp.concatenate(
        [
            grad_query.astype(jnp.bfloat16),
            grad_forget.astype(jnp.bfloat16),
            grad_value.astype(jnp.bfloat16),
            grad_outgate.astype(jnp.bfloat16),
            grad_output_t.astype(jnp.bfloat16),
        ],
        axis=1,
    )
    attn_red = spread_sum(attn_grads, "dp", 32)
    d_normed = row_sum(
        times_trans(d_query, wq_all)
        + times_trans(d_forget, wf_all)
        + times_trans(d_value, wv_all)
        + times_trans(d_outgate, wg_all)
    )
    grad_attn = jnp.sum(d_normed * resid_in * scale_one, axis=0)
    inner_one = jnp.mean(d_normed * attn_full * resid_in, axis=-1, keepdims=True)
    grad_tokens = (
        d_resid + d_normed * attn_full * scale_one - resid_in * scale_one**3 * inner_one
    ).reshape(tokens.shape)
    floor_vector = lax.dynamic_update_slice(
        jnp.zeros((model_width,), jnp.float32), d_floor.reshape(-1), (part_index * local_width,)
    )
    reduced_small = small_sum(jnp.stack([grad_attn, floor_vector, grad_mlp]))
    return (
        layer_out,
        grad_tokens,
        reduced_small[0],
        reduced_small[1],
        attn_red[:, 0 * local_width : 1 * local_width],
        attn_red[:, 1 * local_width : 2 * local_width],
        attn_red[:, 2 * local_width : 3 * local_width],
        attn_red[:, 3 * local_width : 4 * local_width],
        attn_red[:, 4 * local_width : 5 * local_width].T,
        reduced_small[2],
        mlp_red[:, 0:hidden_width],
        mlp_red[:, hidden_width : 2 * hidden_width],
        mlp_red[:, 2 * hidden_width : 3 * hidden_width].T,
    )


def solution(mesh):
    return jax.shard_map(
        shards,
        mesh=mesh,
        in_specs=(
            P("dp", "tensor", None, None),
            P("dp", None, None),
            P(("dp", "tensor")),
            P(("dp", "tensor")),
            P("dp", "tensor"),
            P("dp", "tensor"),
            P("dp", "tensor"),
            P("dp", "tensor"),
            P("tensor", "dp"),
            P(("dp", "tensor")),
            P("dp", "tensor"),
            P("dp", "tensor"),
            P("tensor", "dp"),
            P("dp", "tensor", None, None),
        ),
        out_specs=(
            P("dp", "tensor", None, None),
            P("dp", "tensor", None, None),
            P(("dp", "tensor")),
            P(("dp", "tensor")),
            P("dp", "tensor"),
            P("dp", "tensor"),
            P("dp", "tensor"),
            P("dp", "tensor"),
            P("tensor", "dp"),
            P(("dp", "tensor")),
            P("dp", "tensor"),
            P("dp", "tensor"),
            P("tensor", "dp"),
        ),
        check_vma=False,
    )
```

profile of v0, /device:TPU:0, one launch (start us, length us, event | category | flops | bytes accessed | tf_op | source)
XLA Modules:
  0.0 807.6 jit_solution(461497468060412222)
XLA Ops:
  15.1 11.1 %all-to-all-start = ((f32[128,3,16]{2,1,0:T(4,128)}), f32[128,3,16]{2,1,0:T(4,128)S(1)}, u32[]{:S(2)}, u32[]{:S(2)}) async-start(f32[128,3,16]{2,1,0:T(4,128)} %broadcast_in_dim.29), calls=%async_computation | async-start | bytes 524288 | tf_op jit(solution)/shard_map/all_to_all | solution.py:85
  27.1 11.5 %all-to-all-done = f32[128,3,16]{2,1,0:T(4,128)S(1)} async-done(((f32[128,3,16]{2,1,0:T(4,128)}), f32[128,3,16]{2,1,0:T(4,128)S(1)}, u32[]{:S(2)}, u32[]{:S(2)}) %all-to-all-start) | async-done | bytes 24608 | tf_op jit(solution)/shard_map/all_to_all | solution.py:85
  40.2 15.4 %collective-permute-done = bf16[128,2048]{1,0:T(8,128)(2,1)S(1)} collective-permute-done((bf16[128,2048]{1,0:T(8,128)(2,1)S(1)}, bf16[128,2048]{1,0:T(8,128)(2,1)S(1)}, u32[]{:S(2)}, u32[]{:S(2)}) %collective-permute-start) | collective-permute-done | bytes 524320 | tf_op jit(solution)/shard_map/ppermute | solution.py:62
  58.6 2.8 pad_maximum_fusion.1
  61.4 72.5 %all-gather.3.cloned.1.call-done = bf16[2048,2560]{1,0:T(8,128)(2,1)} async-done(((bf16[64,2560]{1,0:T(8,128)(2,1)}), bf16[2048,2560]{1,0:T(8,128)(2,1)}) %all-gather.3.cloned.1.call-update) | async-done | bytes 10485776 | tf_op jit(solution)/shard_map/all_gather | solution.py:129
  133.9 5.3 slice_bitcast_fusion
  139.2 4.1 copy.78
  143.3 4.1 copy.80
  149.8 3.6 fusion.56
  160.5 2.9 fusion.25
  167.5 5.4 fusion.74
  172.9 3.1 fusion.29
  176.4 4.1 collective-permute-done.2
  182.8 26.3 %collective-permute-done.3 = f32[128,2048]{1,0:T(8,128)} collective-permute-done((f32[128,2048]{1,0:T(8,128)S(1)}, f32[128,2048]{1,0:T(8,128)}, u32[]{:S(2)}, u32[]{:S(2)}) %collective-permute-start.3) | collective-permute-done | bytes 1048608 | tf_op jit(solution)/shard_map/ppermute | solution.py:73
  211.9 13.1 %collective-permute-done.8 = bf16[128,2048]{1,0:T(8,128)(2,1)} collective-permute-done((bf16[128,2048]{1,0:T(8,128)(2,1)S(1)}, bf16[128,2048]{1,0:T(8,128)(2,1)}, u32[]{:S(2)}, u32[]{:S(2)}) %collective-permute-start.8) | collective-permute-done | bytes 524320 | tf_op jit(solution)/shard_map/ppermute | solution.py:62
  226.3 20.7 %collective-permute-done.4 = bf16[128,2048]{1,0:T(8,128)(2,1)S(1)} collective-permute-done((bf16[128,2048]{1,0:T(8,128)(2,1)S(1)}, bf16[128,2048]{1,0:T(8,128)(2,1)S(1)}, u32[]{:S(2)}, u32[]{:S(2)}) %collective-permute-start.4) | collective-permute-done | bytes 524320 | tf_op jit(solution)/shard_map/ppermute | solution.py:62
  251.4 63.5 %all-gather.5.cloned.1.call-done = bf16[2048,4224]{1,0:T(8,128)(2,1)} async-done(((bf16[64,4224]{1,0:T(8,128)(2,1)}), bf16[2048,4224]{1,0:T(8,128)(2,1)}) %all-gather.5.cloned.1.call-update) | async-done | bytes 17301520 | tf_op jit(solution)/shard_map/all_gather | solution.py:130
  315.0 7.0 fusion
  323.9 3.4 fusion.6
  327.3 7.3 multiply_convert_fusion.1
  334.7 3.5 convolution_convert_fusion
  338.2 3.5 convolution_convert_fusion.1
  341.6 3.5 convolution_convert_fusion.2
  345.1 7.9 pad_maximum_fusion
  353.0 21.9 %copy.106 = bf16[2048,4224]{1,0:T(8,128)(2,1)} copy(bf16[2048,4224]{0,1:T(8,128)(2,1)} %pad_maximum_fusion) | data formatting | bytes 34603008
  374.9 6.0 fusion.4
  381.0 5.6 fusion.12
  387.9 5.5 fusion.2
  394.5 3.4 collective-permute-done.6
  398.6 29.0 %collective-permute-done.11 = f32[128,2048]{1,0:T(8,128)S(1)} collective-permute-done((f32[128,2048]{1,0:T(8,128)S(1)}, f32[128,2048]{1,0:T(8,128)S(1)}, u32[]{:S(2)}, u32[]{:S(2)}) %collective-permute-start.11) | collective-permute-done | bytes 1048608 | tf_op jit(solution)/shard_map/ppermute | solution.py:73
  428.1 29.3 %collective-permute-done.7 = f32[128,2048]{1,0:T(8,128)S(1)} collective-permute-done((f32[128,2048]{1,0:T(8,128)S(1)}, f32[128,2048]{1,0:T(8,128)S(1)}, u32[]{:S(2)}, u32[]{:S(2)}) %collective-permute-start.7) | collective-permute-done | bytes 1048608 | tf_op jit(solution)/shard_map/ppermute | solution.py:73
  459.6 17.0 %collective-permute-done.12 = bf16[128,2048]{1,0:T(8,128)(2,1)S(1)} collective-permute-done((bf16[128,2048]{1,0:T(8,128)(2,1)S(1)}, bf16[128,2048]{1,0:T(8,128)(2,1)S(1)}, u32[]{:S(2)}, u32[]{:S(2)}) %collective-permute-start.12) | collective-permute-done | bytes 524320 | tf_op jit(solution)/shard_map/ppermute | solution.py:62
  477.1 2.6 collective-permute-done.13
  480.0 4.7 fusion.76
  487.6 3.2 fusion.59
  492.1 3.3 convolution_select_fusion
  510.0 4.2 fusion.19
  518.6 4.4 fusion.18
  523.0 2.7 fusion.17
  525.7 2.7 fusion.16
  528.4 21.0 %collective-permute-done.15 = f32[128,2048]{1,0:T(8,128)} collective-permute-done((f32[128,2048]{1,0:T(8,128)S(1)}, f32[128,2048]{1,0:T(8,128)}, u32[]{:S(2)}, u32[]{:S(2)}) %collective-permute-start.15) | collective-permute-done | bytes 1048608 | tf_op jit(solution)/shard_map/ppermute | solution.py:73
  552.6 7.2 all-to-all-start.1
  559.8 4.2 fusion.15
  564.0 13.9 %copy.92 = bf16[2048,2560]{1,0:T(8,128)(2,1)} copy(bf16[2048,2560]{0,1:T(8,128)(2,1)} %fusion.15) | data formatting | bytes 20971520 | tf_op jit(solution)/shard_map/concatenate | solution.py:206
  578.0 9.8 %all-to-all-start.2 = ((bf16[32,64,2560]{2,1,0:T(8,128)(2,1)}), bf16[32,64,2560]{2,1,0:T(8,128)(2,1)}, u32[]{:S(2)}, u32[]{:S(2)}) async-start(bf16[32,64,2560]{2,1,0:T(8,128)(2,1)} %bitcast.265), calls=%async_computation.2 | async-start | bytes 20971520 | tf_op jit(solution)/shard_map/all_to_all | solution.py:78
  589.7 163.9 %all-to-all-done.2 = bf16[32,64,2560]{2,1,0:T(8,128)(2,1)} async-done(((bf16[32,64,2560]{2,1,0:T(8,128)(2,1)}), bf16[32,64,2560]{2,1,0:T(8,128)(2,1)}, u32[]{:S(2)}, u32[]{:S(2)}) %all-to-all-start.2) | async-done | bytes 10485792 | tf_op jit(solution)/shard_map/all_to_all | solution.py:78
  753.7 5.8 convert_reduce_fusion
  760.3 31.9 %reduce-scatter.4.cloned.1.call-done = bf16[64,4224]{1,0:T(8,128)(2,1)} async-done(((bf16[2048,4224]{1,0:T(8,128)(2,1)}), bf16[64,4224]{1,0:T(8,128)(2,1)}) %reduce-scatter.4.cloned.1.call-update) | async-done | bytes 540688
  (210 shorter events, 83.6 us)
Async XLA Ops:
  7.2 48.7 %copy-start = (s32[1,4,128]{2,1,0:T(4,128)S(1)}, s32[1,4,128]{2,1,0:T(4,128)}, u32[]{:S(2)}) copy-start(s32[1,4,128]{2,1,0:T(4,128)} %param.16) | copy-start | bytes 6148
  7.2 7.2 copy-start.32
  7.2 7.2 copy-start.33
  7.2 7.2 copy-start.34
  7.2 19.1 %copy-start.3 = (bf16[1,1,128,2048]{3,2,1,0:T(8,128)(2,1)S(1)}, bf16[1,1,128,2048]{3,2,1,0:T(8,128)(2,1)}, u32[]{:S(2)}) copy-start(bf16[1,1,128,2048]{3,2,1,0:T(8,128)(2,1)} %param.15) | copy-start | bytes 1572868
  7.2 126.6 %all-gather.3.cloned.1.call-start = ((), (), s32[]{:S(2)}) async-start(), calls=%async_computation.4 | async-start | bytes 10813440 | tf_op jit(solution)/shard_map/all_gather | solution.py:129
  12.3 302.7 %all-gather.5.cloned.1.call-start = ((), (), s32[]{:S(2)}) async-start(), calls=%async_computation.5 | async-start | bytes 17842176 | tf_op jit(solution)/shard_map/all_gather | solution.py:130
  15.1 23.4 %all-to-all-start = ((f32[128,3,16]{2,1,0:T(4,128)}), f32[128,3,16]{2,1,0:T(4,128)S(1)}, u32[]{:S(2)}, u32[]{:S(2)}) async-start(f32[128,3,16]{2,1,0:T(4,128)} %broadcast_in_dim.29), calls=%async_computation | async-start | bytes 524288 | tf_op jit(solution)/shard_map/all_to_all | solution.py:85
  26.3 765.9 %reduce-scatter.4.cloned.1.call-start = ((), (), s32[]{:S(2)}) async-start(), calls=%async_computation.6 | async-start | bytes 17842176
  27.1 28.7 %copy-start.29 = (f32[128]{0:T(128)}, f32[128]{0:T(128)S(1)}, u32[]{:S(2)}) copy-start(f32[128]{0:T(128)S(1)} %get-tuple-element.105) | copy-start | bytes 1540
  39.2 16.6 %copy-start.27 = (f32[2048]{0:T(1024)}, f32[2048]{0:T(1024)S(1)}, u32[]{:S(2)}) copy-start(f32[2048]{0:T(1024)S(1)} %mul.250) | copy-start | bytes 24580
  39.2 16.7 %copy-start.35 = (s32[4]{0:T(128)S(1)}, s32[4]{0:T(128)}, u32[]{:S(2)}) copy-start(s32[4]{0:T(128)} %constant.52.clone) | copy-start | bytes 52
  39.4 16.3 %collective-permute-start = (bf16[128,2048]{1,0:T(8,128)(2,1)S(1)}, bf16[128,2048]{1,0:T(8,128)(2,1)S(1)}, u32[]{:S(2)}, u32[]{:S(2)}) collective-permute-start(bf16[128,2048]{1,0:T(8,128)(2,1)S(1)} %fusion.62), channel_id=1, source_target_pairs={{0,2},{2,0},{1,3},{3,1},{4,6},{6,4},{5,7},{7,5},{8,10},{10,8},{9,1... | collective-permute-start | bytes 1572872 | tf_op jit(solution)/shard_map/ppermute | solution.py:62
  55.7 5.8 copy-start.20
  55.8 2.9 collective-permute-start.1
  149.8 4.5 copy-start.21
  153.4 4.6 copy-start.6
  176.3 5.6 copy-start.8
  176.3 4.2 collective-permute-start.2
  180.7 28.5 %collective-permute-start.3 = (f32[128,2048]{1,0:T(8,128)S(1)}, f32[128,2048]{1,0:T(8,128)}, u32[]{:S(2)}, u32[]{:S(2)}) collective-permute-start(f32[128,2048]{1,0:T(8,128)S(1)} %fusion.88), channel_id=1, source_target_pairs={{0,2},{2,0},{1,3},{3,1},{4,6},{6,4},{5,7},{7,5},{8,10},{10,8},{9,1... | collective-permute-start | bytes 3145736 | tf_op jit(solution)/shard_map/ppermute | solution.py:73
  181.9 43.1 %collective-permute-start.8 = (bf16[128,2048]{1,0:T(8,128)(2,1)S(1)}, bf16[128,2048]{1,0:T(8,128)(2,1)}, u32[]{:S(2)}, u32[]{:S(2)}) collective-permute-start(bf16[128,2048]{1,0:T(8,128)(2,1)S(1)} %bitcast.268), channel_id=1, source_target_pairs={{0,2},{2,0},{1,3},{3,1},{4,6},{6,4},{5,7},{7,5},{8,10},{10,8},{9,1... | collective-permute-start | bytes 1572872 | tf_op jit(solution)/shard_map/ppermute | solution.py:62
  211.6 35.5 %collective-permute-start.4 = (bf16[128,2048]{1,0:T(8,128)(2,1)S(1)}, bf16[128,2048]{1,0:T(8,128)(2,1)S(1)}, u32[]{:S(2)}, u32[]{:S(2)}) collective-permute-start(bf16[128,2048]{1,0:T(8,128)(2,1)S(1)} %multiply_convert_fusion.4), channel_id=1, source_target_pairs={{0,2},{2,0},{1,3},{3,1},{4,6},{6,4},{5,7},{7,5},{8,10},{10,8},{9,1... | collective-permute-start | bytes 1572872 | tf_op jit(solution)/shard_map/ppermute | solution.py:62
  226.1 21.1 %collective-permute-start.9 = (bf16[2,128,2048]{2,1,0:T(8,128)(2,1)S(1)}, bf16[2,128,2048]{2,1,0:T(8,128)(2,1)S(1)}, u32[]{:S(2)}, u32[]{:S(2)}) collective-permute-start(bf16[2,128,2048]{2,1,0:T(8,128)(2,1)S(1)} %pad_maximum_fusion.7), channel_id=1, source_target_pairs={{0,1},{1,0},{2,3},{3,2},{4,5},{5,4},{6,7},{7,6},{8,9},{9,8},{10,11... | collective-permute-start | bytes 3145736 | tf_op jit(solution)/shard_map/ppermute | solution.py:64
  247.1 2.7 collective-permute-start.5
  315.0 7.0 copy-start.17
  315.0 8.9 %copy-start.36 = (bf16[2048,4224]{1,0:T(8,128)(2,1)S(1)}, bf16[2048,4224]{1,0:T(8,128)(2,1)}, u32[]{:S(2)}) copy-start(bf16[2048,4224]{1,0:T(8,128)(2,1)} %all-gather.5.cloned.1.call-done) | copy-start | bytes 51904516
  327.3 7.4 copy-start.16
  334.7 7.0 copy-start.37
  374.9 6.0 copy-start.38
  386.8 6.9 collective-permute-start.10
  393.6 4.2 collective-permute-start.6
  393.8 33.8 %collective-permute-start.11 = (f32[128,2048]{1,0:T(8,128)S(1)}, f32[128,2048]{1,0:T(8,128)S(1)}, u32[]{:S(2)}, u32[]{:S(2)}) collective-permute-start(f32[128,2048]{1,0:T(8,128)S(1)} %fusion.80), channel_id=1, source_target_pairs={{0,2},{2,0},{1,3},{3,1},{4,6},{6,4},{5,7},{7,5},{8,10},{10,8},{9,1... | collective-permute-start | bytes 3145736 | tf_op jit(solution)/shard_map/ppermute | solution.py:73
  398.0 59.4 %collective-permute-start.7 = (f32[128,2048]{1,0:T(8,128)S(1)}, f32[128,2048]{1,0:T(8,128)S(1)}, u32[]{:S(2)}, u32[]{:S(2)}) collective-permute-start(f32[128,2048]{1,0:T(8,128)S(1)} %fusion.83), channel_id=1, source_target_pairs={{0,2},{2,0},{1,3},{3,1},{4,6},{6,4},{5,7},{7,5},{8,10},{10,8},{9,1... | collective-permute-start | bytes 3145736 | tf_op jit(solution)/shard_map/ppermute | solution.py:73
  459.1 17.6 %collective-permute-start.12 = (bf16[128,2048]{1,0:T(8,128)(2,1)S(1)}, bf16[128,2048]{1,0:T(8,128)(2,1)S(1)}, u32[]{:S(2)}, u32[]{:S(2)}) collective-permute-start(bf16[128,2048]{1,0:T(8,128)(2,1)S(1)} %get-tuple-element.75), channel_id=1, source_target_pairs={{0,2},{2,0},{1,3},{3,1},{4,6},{6,4},{5,7},{7,5},{8,10},{10,8},{9,1... | collective-permute-start | bytes 1572872 | tf_op jit(solution)/shard_map/ppermute | solution.py:62
  476.8 3.0 collective-permute-start.13
  479.9 4.8 copy-start.15
  495.5 6.5 slice-start
  497.4 4.5 slice-start.1
  509.9 4.5 collective-permute-start.14
  516.1 33.3 %collective-permute-start.15 = (f32[128,2048]{1,0:T(8,128)S(1)}, f32[128,2048]{1,0:T(8,128)}, u32[]{:S(2)}, u32[]{:S(2)}) collective-permute-start(f32[128,2048]{1,0:T(8,128)S(1)} %fusion.77), channel_id=1, source_target_pairs={{0,2},{2,0},{1,3},{3,1},{4,6},{6,4},{5,7},{7,5},{8,10},{10,8},{9,1... | collective-permute-start | bytes 3145736 | tf_op jit(solution)/shard_map/ppermute | solution.py:73
  525.7 23.7 %copy-start.28 = (f32[2048]{0:T(1024)S(1)}, f32[2048]{0:T(1024)}, u32[]{:S(2)}) copy-start(f32[2048]{0:T(1024)} %copy-done.27) | copy-start | bytes 24580
  525.7 23.7 %copy-start.30 = (f32[128]{0:T(128)S(1)}, f32[128]{0:T(128)}, u32[]{:S(2)}) copy-start(f32[128]{0:T(128)} %copy-done.29) | copy-start | bytes 1540
  528.4 31.4 %copy-start.23 = (bf16[512,512]{1,0:T(8,128)(2,1)S(1)}, bf16[512,512]{1,0:T(8,128)(2,1)}, u32[]{:S(2)}) copy-start(bf16[512,512]{1,0:T(8,128)(2,1)} %copy-done.22) | copy-start | bytes 1572868
  552.6 25.4 %all-to-all-start.1 = ((f32[128,3,16]{2,1,0:T(4,128)}), f32[128,3,16]{2,1,0:T(4,128)S(1)}, u32[]{:S(2)}, u32[]{:S(2)}) async-start(f32[128,3,16]{2,1,0:T(4,128)} %copy.91), calls=%async_computation.1 | async-start | bytes 524288 | tf_op jit(solution)/shard_map/all_to_all | solution.py:92
  577.9 9.8 %copy-start.10 = (f32[128,2048]{1,0:T(8,128)S(1)}, f32[128,2048]{1,0:T(8,128)}, u32[]{:S(2)}) copy-start(f32[128,2048]{1,0:T(8,128)} %get-tuple-element.76) | copy-start | bytes 3145732
  578.0 9.8 %copy-start.31 = (f32[128]{0:T(128)S(1)}, f32[128]{0:T(128)}, u32[]{:S(2)}) copy-start(f32[128]{0:T(128)} %get-tuple-element.104) | copy-start | bytes 1540
  578.0 175.7 %all-to-all-start.2 = ((bf16[32,64,2560]{2,1,0:T(8,128)(2,1)}), bf16[32,64,2560]{2,1,0:T(8,128)(2,1)}, u32[]{:S(2)}, u32[]{:S(2)}) async-start(bf16[32,64,2560]{2,1,0:T(8,128)(2,1)} %bitcast.265), calls=%async_computation.2 | async-start | bytes 20971520 | tf_op jit(solution)/shard_map/all_to_all | solution.py:78
  795.3 5.3 copy-start.1
  (20 other events, 51.6 us)
Sparse Core Ops, SparseCore 0:
  12.4 121.4 all-gather.2
  136.9 177.9 all-gather.4
  375.0 417.0 reduce-scatter.3
where the time goes:
time: 813 us; the launch traced here: 808 us
  waiting for transfers between devices  527 us (65%)
  matrix products  108 us (13%)
  local copies, waits for them, and re-layouts  86.1 us (11%)
  other arithmetic  37 us (5%)
  starting transfers between devices  34 us (4%)
  between operations  15.3 us (2%)
    all_to_all x1, waiting for transfers between devices, spread_sum(): got = lax.all_to_all(blocks, axis, 0, 0, tiled=False)  164 us
    ppermute x4, waiting for transfers between devices, row_sum(): return mine + lax.ppermute(theirs, 'tensor', ACROSS)  106 us
    all_gather x1, waiting for transfers between devices, shards(): attn_all = lax.all_gather(attn_pack, 'dp', axis=0, tiled=True)  72.5 us
    ppermute x4, waiting for transfers between devices, row_gather(): across = lax.ppermute(values, 'tensor', ACROSS)  66.2 us
    all_gather x1, waiting for transfers between devices, shards(): mlp_all = lax.all_gather(mlp_pack, 'dp', axis=0, tiled=True)  63.5 us
    unnamed x101, local copies, waits for them, and re-layouts  40.4 us
    dot_general x8, matrix products, matmul_plain(): return jnp.dot(left, right, preferred_element_type=jnp.float32)  36.9 us
    unnamed x4, waiting for transfers between devices  31.9 us
  transfers between devices with their start and end apart: 22, of which 19 were waited for; matrix products, arithmetic and copies ran while one was open for 19% of the time, Pallas kernels for 0%

commit v1 on v0

--- a/solution.py
+++ b/solution.py
@@ -126,8 +126,10 @@
     cot_local = cotangent[0].reshape(-1, model_width)
     attn_pack = jnp.concatenate([w_query, w_forget, w_value, w_outgate, w_output.T], axis=1)
     mlp_pack = jnp.concatenate([w_gate, w_up, w_down.T], axis=1)
-    attn_all = lax.all_gather(attn_pack, "dp", axis=0, tiled=True)
-    mlp_all = lax.all_gather(mlp_pack, "dp", axis=0, tiled=True)
+    block_now = jax.lax.all_gather(
+        jnp.concatenate([attn_pack, mlp_pack], axis=1), "dp", axis=0, tiled=True
+    )
+    attn_all, mlp_all = jnp.split(block_now, [attn_pack.shape[1]], axis=1)
     wq_all = attn_all[:, 0 * local_width : 1 * local_width]
     wf_all = attn_all[:, 1 * local_width : 2 * local_width]
     wv_all = attn_all[:, 2 * local_width : 3 * local_width]

time: 813 us -> 844 us (1.038)
  waiting for transfers between devices: 527 us -> 555 us
    all_gather x2 -> x1, waiting for transfers between devices: 136 us -> 184 us  [shards(): jax.lax.all_gather(jnp.concatenate([attn_pack, mlp_pack], axis=1), 'dp',...]
    ppermute x4, waiting for transfers between devices: 106 us -> 80.8 us  [row_sum(): return mine + lax.ppermute(theirs, 'tensor', ACROSS)]
    ppermute x4, waiting for transfers between devices: 66.2 us -> 78 us  [row_gather(): across = lax.ppermute(values, 'tensor', ACROSS)]
    all_to_all x1, waiting for transfers between devices: 164 us -> 153 us  [spread_sum(): got = lax.all_to_all(blocks, axis, 0, 0, tiled=False)]
    unnamed x4 -> x3, waiting for transfers between devices: 31.9 us -> 37.6 us
    unnamed x101 -> x98, local copies, waits for them, and re-layouts: 40.4 us -> 36.2 us
  transfers between devices with their start and end apart: 22 -> 21, of which waited for: 19 -> 16; matrix products, arithmetic and copies ran while one was open for 19% -> 14% of each run, Pallas kernels for 0% -> 0%
where the time goes in v1:
time: 844 us; the launch traced here: 839 us
  waiting for transfers between devices  555 us (66%)
  matrix products  116 us (14%)
  local copies, waits for them, and re-layouts  83.1 us (10%)
  starting transfers between devices  36.4 us (4%)
  other arithmetic  32.5 us (4%)
  between operations  15.5 us (2%)
    all_gather x1, waiting for transfers between devices, shards(): jax.lax.all_gather(jnp.concatenate([attn_pack, mlp_pack], axis=1), 'dp',...  184 us
    all_to_all x1, waiting for transfers between devices, spread_sum(): got = lax.all_to_all(blocks, axis, 0, 0, tiled=False)  153 us
    ppermute x4, waiting for transfers between devices, row_sum(): return mine + lax.ppermute(theirs, 'tensor', ACROSS)  80.8 us
    ppermute x4, waiting for transfers between devices, row_gather(): across = lax.ppermute(values, 'tensor', ACROSS)  78 us
    unnamed x3, waiting for transfers between devices  37.6 us
    dot_general x8, matrix products, matmul_plain(): return jnp.dot(left, right, preferred_element_type=jnp.float32)  37.3 us
    unnamed x98, local copies, waits for them, and re-layouts  36.2 us
    dot_general x8, matrix products, times_trans(): lax.dot_general(left, right, (((1,), (1,)), ((), ())), preferred_element_...  32 us
  transfers between devices with their start and end apart: 21, of which 16 were waited for; matrix products, arithmetic and copies ran while one was open for 14% of the time, Pallas kernels for 0%

profile of v1, /device:TPU:0, one launch (start us, length us, event | category | flops | bytes accessed | tf_op | source)
XLA Modules:
  0.0 838.7 jit_solution(9228379636467242084)
XLA Ops:
  16.1 11.1 %all-to-all-start = ((f32[128,3,16]{2,1,0:T(4,128)}), f32[128,3,16]{2,1,0:T(4,128)S(1)}, u32[]{:S(2)}, u32[]{:S(2)}) async-start(f32[128,3,16]{2,1,0:T(4,128)} %broadcast_in_dim.29), calls=%async_computation | async-start | bytes 524288 | tf_op jit(solution)/shard_map/all_to_all | solution.py:85
  28.0 10.1 %all-to-all-done = f32[128,3,16]{2,1,0:T(4,128)S(1)} async-done(((f32[128,3,16]{2,1,0:T(4,128)}), f32[128,3,16]{2,1,0:T(4,128)S(1)}, u32[]{:S(2)}, u32[]{:S(2)}) %all-to-all-start) | async-done | bytes 24608 | tf_op jit(solution)/shard_map/all_to_all | solution.py:85
  39.9 13.3 %collective-permute-done = bf16[128,2048]{1,0:T(8,128)(2,1)S(1)} collective-permute-done((bf16[128,2048]{1,0:T(8,128)(2,1)S(1)}, bf16[128,2048]{1,0:T(8,128)(2,1)S(1)}, u32[]{:S(2)}, u32[]{:S(2)}) %collective-permute-start) | collective-permute-done | bytes 524320 | tf_op jit(solution)/shard_map/ppermute | solution.py:62
  56.1 2.9 pad_maximum_fusion.1
  59.0 184.0 %all-gather.2.cloned.1.call-done = bf16[2048,6784]{1,0:T(8,128)(2,1)} async-done(((bf16[64,6784]{1,0:T(8,128)(2,1)}), bf16[2048,6784]{1,0:T(8,128)(2,1)}) %all-gather.2.cloned.1.call-update) | async-done | bytes 27787280 | tf_op jit(solution)/shard_map/all_gather | solution.py:129
  243.1 5.3 slice_bitcast_fusion
  248.3 4.2 copy.78
  252.5 3.9 copy.80
  259.0 3.6 fusion.56
  268.7 2.9 fusion.25
  271.6 2.9 convolution_bitcast_fusion.2
  277.0 4.8 fusion.74
  281.8 3.1 fusion.29
  285.3 4.1 collective-permute-done.2
  293.2 34.5 %collective-permute-done.8 = bf16[128,2048]{1,0:T(8,128)(2,1)S(1)} collective-permute-done((bf16[128,2048]{1,0:T(8,128)(2,1)S(1)}, bf16[128,2048]{1,0:T(8,128)(2,1)S(1)}, u32[]{:S(2)}, u32[]{:S(2)}) %collective-permute-start.8) | collective-permute-done | bytes 524320 | tf_op jit(solution)/shard_map/ppermute | solution.py:62
  331.4 13.0 %collective-permute-done.4 = bf16[128,2048]{1,0:T(8,128)(2,1)S(1)} collective-permute-done((bf16[128,2048]{1,0:T(8,128)(2,1)S(1)}, bf16[128,2048]{1,0:T(8,128)(2,1)S(1)}, u32[]{:S(2)}, u32[]{:S(2)}) %collective-permute-start.4) | collective-permute-done | bytes 524320 | tf_op jit(solution)/shard_map/ppermute | solution.py:62
  344.8 5.8 fusion
  350.8 5.8 fusion.6
  356.6 7.2 multiply_convert_fusion.1
  363.8 3.5 convolution_convert_fusion
  367.3 3.5 convolution_convert_fusion.1
  370.8 3.5 convolution_convert_fusion.2
  374.2 7.9 pad_maximum_fusion
  382.1 21.3 %copy.106 = bf16[2048,4224]{1,0:T(8,128)(2,1)} copy(bf16[2048,4224]{0,1:T(8,128)(2,1)} %pad_maximum_fusion) | data formatting | bytes 34603008
  403.4 6.0 fusion.4
  409.4 5.5 fusion.12
  416.4 5.5 fusion.2
  423.4 3.3 collective-permute-done.6
  427.2 29.4 %collective-permute-done.11 = f32[128,2048]{1,0:T(8,128)S(1)} collective-permute-done((f32[128,2048]{1,0:T(8,128)S(1)}, f32[128,2048]{1,0:T(8,128)S(1)}, u32[]{:S(2)}, u32[]{:S(2)}) %collective-permute-start.11) | collective-permute-done | bytes 1048608 | tf_op jit(solution)/shard_map/ppermute | solution.py:73
  457.1 29.1 %collective-permute-done.7 = f32[128,2048]{1,0:T(8,128)S(1)} collective-permute-done((f32[128,2048]{1,0:T(8,128)S(1)}, f32[128,2048]{1,0:T(8,128)S(1)}, u32[]{:S(2)}, u32[]{:S(2)}) %collective-permute-start.7) | collective-permute-done | bytes 1048608 | tf_op jit(solution)/shard_map/ppermute | solution.py:73
  488.1 17.2 %collective-permute-done.12 = bf16[128,2048]{1,0:T(8,128)(2,1)S(1)} collective-permute-done((bf16[128,2048]{1,0:T(8,128)(2,1)S(1)}, bf16[128,2048]{1,0:T(8,128)(2,1)S(1)}, u32[]{:S(2)}, u32[]{:S(2)}) %collective-permute-start.12) | collective-permute-done | bytes 524320 | tf_op jit(solution)/shard_map/ppermute | solution.py:62
  508.6 4.7 fusion.76
  516.2 3.2 fusion.59
  520.8 3.3 convolution_select_fusion
  530.5 2.9 fusion.38
  533.5 2.9 fusion.36
  536.4 2.9 fusion.34
  539.3 3.0 add_add_fusion
  546.0 4.3 fusion.19
  554.3 4.4 fusion.18
  564.1 22.4 %collective-permute-done.15 = f32[128,2048]{1,0:T(8,128)} collective-permute-done((f32[128,2048]{1,0:T(8,128)S(1)}, f32[128,2048]{1,0:T(8,128)}, u32[]{:S(2)}, u32[]{:S(2)}) %collective-permute-start.15) | collective-permute-done | bytes 1048608 | tf_op jit(solution)/shard_map/ppermute | solution.py:73
  589.7 7.4 all-to-all-start.1
  597.1 4.2 fusion.15
  601.4 13.9 %copy.92 = bf16[2048,2560]{1,0:T(8,128)(2,1)} copy(bf16[2048,2560]{0,1:T(8,128)(2,1)} %fusion.15) | data formatting | bytes 20971520 | tf_op jit(solution)/shard_map/concatenate | solution.py:208
  615.2 9.8 %all-to-all-start.2 = ((bf16[32,64,2560]{2,1,0:T(8,128)(2,1)}), bf16[32,64,2560]{2,1,0:T(8,128)(2,1)}, u32[]{:S(2)}, u32[]{:S(2)}) async-start(bf16[32,64,2560]{2,1,0:T(8,128)(2,1)} %bitcast.266), calls=%async_computation.2 | async-start | bytes 20971520 | tf_op jit(solution)/shard_map/all_to_all | solution.py:78
  627.0 152.6 %all-to-all-done.2 = bf16[32,64,2560]{2,1,0:T(8,128)(2,1)} async-done(((bf16[32,64,2560]{2,1,0:T(8,128)(2,1)}), bf16[32,64,2560]{2,1,0:T(8,128)(2,1)}, u32[]{:S(2)}, u32[]{:S(2)}) %all-to-all-start.2) | async-done | bytes 10485792 | tf_op jit(solution)/shard_map/all_to_all | solution.py:78
  779.7 5.8 convert_reduce_fusion
  786.3 37.5 %reduce-scatter.4.cloned.1.call-done = bf16[64,4224]{1,0:T(8,128)(2,1)} async-done(((bf16[2048,4224]{1,0:T(8,128)(2,1)}), bf16[64,4224]{1,0:T(8,128)(2,1)}) %reduce-scatter.4.cloned.1.call-update) | async-done | bytes 540688
  (202 shorter events, 79.9 us)
Async XLA Ops:
  7.2 46.2 %copy-start = (s32[1,4,128]{2,1,0:T(4,128)S(1)}, s32[1,4,128]{2,1,0:T(4,128)}, u32[]{:S(2)}) copy-start(s32[1,4,128]{2,1,0:T(4,128)} %param.16) | copy-start | bytes 6148
  7.2 8.1 copy-start.33
  7.2 8.1 copy-start.34
  7.2 8.1 copy-start.35
  7.2 20.1 %copy-start.3 = (bf16[1,1,128,2048]{3,2,1,0:T(8,128)(2,1)S(1)}, bf16[1,1,128,2048]{3,2,1,0:T(8,128)(2,1)}, u32[]{:S(2)}) copy-start(bf16[1,1,128,2048]{3,2,1,0:T(8,128)(2,1)} %param.15) | copy-start | bytes 1572868
  7.2 235.8 %all-gather.2.cloned.1.call-start = ((), (), s32[]{:S(2)}) async-start(), calls=%async_computation.4 | async-start | bytes 28655616 | tf_op jit(solution)/shard_map/all_gather | solution.py:129
  16.1 22.1 %all-to-all-start = ((f32[128,3,16]{2,1,0:T(4,128)}), f32[128,3,16]{2,1,0:T(4,128)S(1)}, u32[]{:S(2)}, u32[]{:S(2)}) async-start(f32[128,3,16]{2,1,0:T(4,128)} %broadcast_in_dim.29), calls=%async_computation | async-start | bytes 524288 | tf_op jit(solution)/shard_map/all_to_all | solution.py:85
  27.3 796.6 %reduce-scatter.4.cloned.1.call-start = ((), (), s32[]{:S(2)}) async-start(), calls=%async_computation.5 | async-start | bytes 17842176
  28.0 25.2 %copy-start.30 = (f32[128]{0:T(128)}, f32[128]{0:T(128)S(1)}, u32[]{:S(2)}) copy-start(f32[128]{0:T(128)S(1)} %get-tuple-element.105) | copy-start | bytes 1540
  38.7 14.6 %copy-start.36 = (s32[4]{0:T(128)S(1)}, s32[4]{0:T(128)}, u32[]{:S(2)}) copy-start(s32[4]{0:T(128)} %constant.52.clone) | copy-start | bytes 52
  38.8 15.2 %copy-start.28 = (f32[2048]{0:T(1024)}, f32[2048]{0:T(1024)S(1)}, u32[]{:S(2)}) copy-start(f32[2048]{0:T(1024)S(1)} %mul.250) | copy-start | bytes 24580
  39.0 14.1 %collective-permute-start = (bf16[128,2048]{1,0:T(8,128)(2,1)S(1)}, bf16[128,2048]{1,0:T(8,128)(2,1)S(1)}, u32[]{:S(2)}, u32[]{:S(2)}) collective-permute-start(bf16[128,2048]{1,0:T(8,128)(2,1)S(1)} %fusion.62), channel_id=1, source_target_pairs={{0,2},{2,0},{1,3},{3,1},{4,6},{6,4},{5,7},{7,5},{8,10},{10,8},{9,1... | collective-permute-start | bytes 1572872 | tf_op jit(solution)/shard_map/ppermute | solution.py:62
  53.1 5.9 copy-start.19
  53.2 2.9 collective-permute-start.1
  259.0 4.6 copy-start.18
  259.0 4.6 copy-start.20
  262.6 3.5 copy-start.6
  271.6 5.5 copy-start.9
  284.9 5.8 copy-start.2
  285.2 6.5 copy-start.8
  285.2 4.2 collective-permute-start.2
  290.7 37.8 %collective-permute-start.3 = (f32[128,2048]{1,0:T(8,128)}, f32[128,2048]{1,0:T(8,128)}, u32[]{:S(2)}, u32[]{:S(2)}) collective-permute-start(f32[128,2048]{1,0:T(8,128)} %fusion.88), channel_id=1, source_target_pairs={{0,2},{2,0},{1,3},{3,1},{4,6},{6,4},{5,7},{7,5},{8,10},{10,8},{9,1... | collective-permute-start | bytes 3145736 | tf_op jit(solution)/shard_map/ppermute | solution.py:73
  291.6 36.0 %collective-permute-start.8 = (bf16[128,2048]{1,0:T(8,128)(2,1)S(1)}, bf16[128,2048]{1,0:T(8,128)(2,1)S(1)}, u32[]{:S(2)}, u32[]{:S(2)}) collective-permute-start(bf16[128,2048]{1,0:T(8,128)(2,1)S(1)} %bitcast.267), channel_id=1, source_target_pairs={{0,2},{2,0},{1,3},{3,1},{4,6},{6,4},{5,7},{7,5},{8,10},{10,8},{9,1... | collective-permute-start | bytes 1572872 | tf_op jit(solution)/shard_map/ppermute | solution.py:62
  293.2 35.3 %copy-start.14 = (f32[2,128,2048]{2,1,0:T(8,128)S(1)}, f32[2,128,2048]{2,1,0:T(8,128)}, u32[]{:S(2)}) copy-start(f32[2,128,2048]{2,1,0:T(8,128)} %copy-done.13) | copy-start | bytes 6291460
  327.8 16.8 %collective-permute-start.9 = (bf16[2,128,2048]{2,1,0:T(8,128)(2,1)S(1)}, bf16[2,128,2048]{2,1,0:T(8,128)(2,1)S(1)}, u32[]{:S(2)}, u32[]{:S(2)}) collective-permute-start(bf16[2,128,2048]{2,1,0:T(8,128)(2,1)S(1)} %pad_maximum_fusion.7), channel_id=1, source_target_pairs={{0,1},{1,0},{2,3},{3,2},{4,5},{5,4},{6,7},{7,6},{8,9},{9,8},{10,11... | collective-permute-start | bytes 3145736 | tf_op jit(solution)/shard_map/ppermute | solution.py:64
  330.6 14.0 %copy-start.22 = (bf16[128,2048]{1,0:T(8,128)(2,1)S(1)}, bf16[128,2048]{1,0:T(8,128)(2,1)}, u32[]{:S(2)}) copy-start(bf16[128,2048]{1,0:T(8,128)(2,1)} %copy-done.21) | copy-start | bytes 1572868
  330.6 13.8 %collective-permute-start.4 = (bf16[128,2048]{1,0:T(8,128)(2,1)S(1)}, bf16[128,2048]{1,0:T(8,128)(2,1)S(1)}, u32[]{:S(2)}, u32[]{:S(2)}) collective-permute-start(bf16[128,2048]{1,0:T(8,128)(2,1)S(1)} %multiply_convert_fusion.4), channel_id=1, source_target_pairs={{0,2},{2,0},{1,3},{3,1},{4,6},{6,4},{5,7},{7,5},{8,10},{10,8},{9,1... | collective-permute-start | bytes 1572872 | tf_op jit(solution)/shard_map/ppermute | solution.py:62
  344.5 6.1 collective-permute-start.5
  363.8 7.0 copy-start.37
  403.4 6.0 copy-start.38
  415.2 7.7 collective-permute-start.10
  422.1 4.6 collective-permute-start.6
  423.0 33.6 %collective-permute-start.11 = (f32[128,2048]{1,0:T(8,128)S(1)}, f32[128,2048]{1,0:T(8,128)S(1)}, u32[]{:S(2)}, u32[]{:S(2)}) collective-permute-start(f32[128,2048]{1,0:T(8,128)S(1)} %fusion.80), channel_id=1, source_target_pairs={{0,2},{2,0},{1,3},{3,1},{4,6},{6,4},{5,7},{7,5},{8,10},{10,8},{9,1... | collective-permute-start | bytes 3145736 | tf_op jit(solution)/shard_map/ppermute | solution.py:73
  426.8 59.3 %collective-permute-start.7 = (f32[128,2048]{1,0:T(8,128)S(1)}, f32[128,2048]{1,0:T(8,128)S(1)}, u32[]{:S(2)}, u32[]{:S(2)}) collective-permute-start(f32[128,2048]{1,0:T(8,128)S(1)} %fusion.83), channel_id=1, source_target_pairs={{0,2},{2,0},{1,3},{3,1},{4,6},{6,4},{5,7},{7,5},{8,10},{10,8},{9,1... | collective-permute-start | bytes 3145736 | tf_op jit(solution)/shard_map/ppermute | solution.py:73
  487.8 17.5 %collective-permute-start.12 = (bf16[128,2048]{1,0:T(8,128)(2,1)S(1)}, bf16[128,2048]{1,0:T(8,128)(2,1)S(1)}, u32[]{:S(2)}, u32[]{:S(2)}) collective-permute-start(bf16[128,2048]{1,0:T(8,128)(2,1)S(1)} %get-tuple-element.75), channel_id=1, source_target_pairs={{0,2},{2,0},{1,3},{3,1},{4,6},{6,4},{5,7},{7,5},{8,10},{10,8},{9,1... | collective-permute-start | bytes 1572872 | tf_op jit(solution)/shard_map/ppermute | solution.py:62
  505.4 3.0 collective-permute-start.13
  508.5 4.8 copy-start.16
  545.9 4.5 collective-permute-start.14
  552.1 34.4 %collective-permute-start.15 = (f32[128,2048]{1,0:T(8,128)S(1)}, f32[128,2048]{1,0:T(8,128)}, u32[]{:S(2)}, u32[]{:S(2)}) collective-permute-start(f32[128,2048]{1,0:T(8,128)S(1)} %fusion.77), channel_id=1, source_target_pairs={{0,2},{2,0},{1,3},{3,1},{4,6},{6,4},{5,7},{7,5},{8,10},{10,8},{9,1... | collective-permute-start | bytes 3145736 | tf_op jit(solution)/shard_map/ppermute | solution.py:73
  554.3 4.4 copy-start.15
  561.4 25.1 %copy-start.29 = (f32[2048]{0:T(1024)S(1)}, f32[2048]{0:T(1024)}, u32[]{:S(2)}) copy-start(f32[2048]{0:T(1024)} %copy-done.28) | copy-start | bytes 24580
  561.4 25.1 %copy-start.31 = (f32[128]{0:T(128)S(1)}, f32[128]{0:T(128)}, u32[]{:S(2)}) copy-start(f32[128]{0:T(128)} %copy-done.30) | copy-start | bytes 1540
  564.1 33.0 %copy-start.24 = (bf16[512,512]{1,0:T(8,128)(2,1)S(1)}, bf16[512,512]{1,0:T(8,128)(2,1)}, u32[]{:S(2)}) copy-start(bf16[512,512]{1,0:T(8,128)(2,1)} %copy-done.23) | copy-start | bytes 1572868
  589.7 25.5 %all-to-all-start.1 = ((f32[128,3,16]{2,1,0:T(4,128)}), f32[128,3,16]{2,1,0:T(4,128)S(1)}, u32[]{:S(2)}, u32[]{:S(2)}) async-start(f32[128,3,16]{2,1,0:T(4,128)} %copy.91), calls=%async_computation.1 | async-start | bytes 524288 | tf_op jit(solution)/shard_map/all_to_all | solution.py:92
  615.2 9.8 %copy-start.10 = (f32[128,2048]{1,0:T(8,128)S(1)}, f32[128,2048]{1,0:T(8,128)}, u32[]{:S(2)}) copy-start(f32[128,2048]{1,0:T(8,128)} %get-tuple-element.76) | copy-start | bytes 3145732
  615.2 9.8 %copy-start.32 = (f32[128]{0:T(128)S(1)}, f32[128]{0:T(128)}, u32[]{:S(2)}) copy-start(f32[128]{0:T(128)} %get-tuple-element.104) | copy-start | bytes 1540
  615.2 164.4 %all-to-all-start.2 = ((bf16[32,64,2560]{2,1,0:T(8,128)(2,1)}), bf16[32,64,2560]{2,1,0:T(8,128)(2,1)}, u32[]{:S(2)}, u32[]{:S(2)}) async-start(bf16[32,64,2560]{2,1,0:T(8,128)(2,1)} %bitcast.266), calls=%async_computation.2 | async-start | bytes 20971520 | tf_op jit(solution)/shard_map/all_to_all | solution.py:78
  827.2 4.1 copy-start.1
  (16 other events, 40.0 us)
Sparse Core Ops, SparseCore 0:
  15.4 227.5 all-gather.1
  403.5 420.2 reduce-scatter.3
